TPU v7x, 256 devices: a whole 4x4x8 slice. The times are simulated.
256 devices in a mesh: dp: 32 (over y, x, core), ind: 8 (over z).
Axes of the slice: x: 4, y: 4, z: 8, core: 2. Of those that a mesh axis runs over, the one named last changes fastest.
Arguments:
- inputs: bfloat16 [65536, 256], P('dp'), may hold values from -6 to 6
- targets: bfloat16 [65536], P('dp'), may hold values from -6 to 6
- row_counts: int32 [32], replicated, may hold values from 1 to 2048, 32768 in all
- w_in: bfloat16 [256, 1024], replicated, may hold values from -0.375 to 0.375
- w_mid: bfloat16 [1024, 1024], replicated, may hold values from -0.1875 to 0.1875
- w_out: bfloat16 [1024, 128], replicated, may hold values from -0.1875 to 0.1875
- feat_gain: float32 [128], replicated, may hold values from 0.1 to 1.9
- inducing: bfloat16 [16384, 128], P('ind'), may hold values from -6 to 6
- log_scale: float32 [1], replicated, may hold values from -0.5 to 0.5
- lengthscale: float32 [1], replicated, may hold values from 3.2 to 3.5
- noise_var: float32 [1], replicated, may hold values from 5e-05 to 0.0002
Outputs:
- panel_factor: float32 [16384, 512], P(('ind', 'dp'))
- rhs_next: float32 [16384], P(('ind', 'dp'))
- panel_solution: float32 [512], replicated
- log_det: float32 [1], replicated
Inputs may be any that keep to these rules, and one draw needn't show every extreme that they name: The first row_counts[s] samples of shard s are valid; the counts sum to 32768 and one shard has all 2048 slots valid.
All inputs are finite; a program needn't handle non-finite values.
Results may differ from a plain program's by a relative error of at most 0.012.
The roundings to bfloat16 on the way count: a program that leaves them out, or rounds other values in their place, can miss the bound.
Values may be sent and summed in bfloat16 or wider, within the bound.
No kernel may reach another device: no remote copies, remote signals or barrier semaphores. Data moves between devices by JAX's collectives and lax.ppermute only.
A program may use at most 64 MiB of HBM per device.

v0:
```python
import jax
import jax.numpy as jnp
from jax import lax
from jax.sharding import PartitionSpec as P

PB = 512


JITTER = 0.0001


def from_root(shard, axis, root):
    mine = lax.axis_index(axis) == root
    return lax.psum(jnp.where(mine, shard, jnp.zeros_like(shard)), axis)


def embed(inputs, w_in, w_mid, w_out, feat_gain):
    hidden_one = jax.nn.gelu(jnp.dot(inputs, w_in, preferred_element_type=jnp.float32)).astype(
        jnp.bfloat16
    )
    hidden_two = jax.nn.gelu(jnp.dot(hidden_one, w_mid, preferred_element_type=jnp.float32)).astype(
        jnp.bfloat16
    )
    projected = jnp.dot(hidden_two, w_out, preferred_element_type=jnp.float32)
    scaled = (
        projected
        * lax.rsqrt(jnp.mean(projected * projected, axis=-1, keepdims=True) + 1e-06)
        * feat_gain
    )
    return scaled.astype(jnp.bfloat16)


def exponent(points, others, scale_log, inverse_sq):
    point_sq = jnp.sum(jnp.square(points.astype(jnp.float32)), axis=1)
    other_sq = jnp.sum(jnp.square(others.astype(jnp.float32)), axis=1)
    cross_term = jnp.dot(points, others.T, preferred_element_type=jnp.float32)
    return (
        scale_log
        - 0.5 * inverse_sq * (point_sq[:, None] + other_sq[None, :])
        + inverse_sq * cross_term
    )


def body(
    inputs,
    targets,
    row_counts,
    w_in,
    w_mid,
    w_out,
    feat_gain,
    inducing,
    log_scale,
    lengthscale,
    noise_var,
):
    shards = lax.axis_size("dp")
    groups = lax.axis_size("ind")
    shard_id = lax.axis_index("dp")
    group_id = lax.axis_index("ind")
    capacity = inputs.shape[0]
    piece_rows = capacity // groups
    block_rows = inducing.shape[0]
    owned_rows = block_rows // shards
    start_row = group_id * piece_rows
    input_piece = lax.dynamic_slice_in_dim(inputs, start_row, piece_rows, 0)
    embedded_piece = embed(input_piece, w_in, w_mid, w_out, feat_gain)
    shard_iota = jnp.arange(shards, dtype=jnp.int32)
    own_count = jnp.sum(jnp.where(shard_iota == shard_id, row_counts, 0))
    embedded = lax.all_gather(embedded_piece, "ind", axis=0, tiled=True)
    valid_rows = jnp.arange(capacity, dtype=jnp.int32) < own_count
    target_used = jnp.where(valid_rows, targets, jnp.zeros((), jnp.bfloat16))
    scale_log = log_scale[0]
    inverse_sq = 1.0 / (lengthscale[0] * lengthscale[0])
    variance = noise_var[0]
    panel_points = from_root(inducing[:PB], "ind", 0)
    panel_kernel = jnp.where(
        valid_rows[None, :], jnp.exp(exponent(panel_points, embedded, scale_log, inverse_sq)), 0.0
    ).astype(jnp.bfloat16)
    block_size = min(512, block_rows)
    grouped = inducing.reshape(block_rows // block_size, block_size, inducing.shape[1])

    def gram_block(points):
        kernel_rows = jnp.exp(exponent(points, embedded, scale_log, inverse_sq)).astype(
            jnp.bfloat16
        )
        return (
            jnp.dot(kernel_rows, panel_kernel.T, preferred_element_type=jnp.float32),
            jnp.dot(kernel_rows, target_used, preferred_element_type=jnp.float32),
        )

    gram_rows, cross_rows = lax.map(gram_block, grouped)
    gram_rows = gram_rows.reshape(block_rows, gram_rows.shape[2])
    cross_rows = cross_rows.reshape(block_rows)
    gram_total, cross_total = lax.psum((gram_rows, cross_rows), "dp")
    gram_own = lax.dynamic_slice_in_dim(gram_total, shard_id * owned_rows, owned_rows, 0)
    cross_own = lax.dynamic_slice_in_dim(cross_total, shard_id * owned_rows, owned_rows, 0)
    own_index = (
        group_id * block_rows + shard_id * owned_rows + jnp.arange(owned_rows, dtype=jnp.int32)
    )
    panel_index = jnp.arange(PB, dtype=jnp.int32)
    own_points = lax.dynamic_slice_in_dim(inducing, shard_id * owned_rows, owned_rows, 0)
    kernel_mm = jnp.exp(exponent(own_points, panel_points, scale_log, inverse_sq)) + jnp.where(
        own_index[:, None] == panel_index[None, :], JITTER, 0.0
    )
    system_rows = kernel_mm + gram_own / variance
    right_side = cross_own / variance
    column_rows, column_right = (
        lax.all_gather(system_rows, "dp", axis=0, tiled=True),
        lax.all_gather(right_side, "dp", axis=0, tiled=True),
    )
    system_top, right_top = (
        from_root(column_rows[:PB], "ind", 0),
        from_root(column_right[:PB], "ind", 0),
    )
    factor_top = jnp.linalg.cholesky(system_top)
    log_det = 2.0 * jnp.sum(jnp.log(jnp.diagonal(factor_top)))
    panel_solution = lax.linalg.triangular_solve(
        factor_top, right_top[:, None], left_side=True, lower=True
    )[:, 0]
    panel_factor = lax.linalg.triangular_solve(
        factor_top, system_rows, left_side=False, lower=True, transpose_a=True
    )
    rhs_next = right_side - jnp.dot(panel_factor, panel_solution, precision=lax.Precision.HIGHEST)
    return (panel_factor, rhs_next, panel_solution, log_det.reshape(1))


def solution(mesh):
    return jax.shard_map(
        body,
        mesh=mesh,
        in_specs=(P("dp", None), P("dp"), P(), P(), P(), P(), P(), P("ind", None), P(), P(), P()),
        out_specs=(P(("ind", "dp"), None), P(("ind", "dp")), P(), P()),
        check_vma=False,
    )
```

profile of v0, /device:TPU:0, one launch (start us, length us, event | category | flops | bytes accessed | tf_op | source)
XLA Modules:
  0.0 630.5 jit_solution(4431157111453220107)
XLA Ops:
  7.2 1.7 slice_select_fusion
  9.0 1.4 fusion.56
  10.5 2.1 multiply_reduce_fusion.4
  12.7 27.6 %all_gather.9 = bf16[2048,128]{0,1:T(8,128)(2,1)S(1)} all-gather(bf16[256,128]{0,1:T(8,128)(2,1)S(1)} %multiply_convert_fusion), channel_id=1, replica_groups=mesh['dp'=32,'ind'=8] {'ind'}, dimensions={0}, use_global_device_ids=true | all-gather | bytes 589824 | tf_op jit(solution)/shard_map/all_gather | solution.py:70
  44.0 40.7 %all-reduce.6.cloned.1.call-done = bf16[512,128]{1,0:T(8,128)(2,1)} async-done(((bf16[512,128]{1,0:T(8,128)(2,1)}), bf16[512,128]{1,0:T(8,128)(2,1)}) %all-reduce.6.cloned.1.call-update) | async-done | bytes 131088 | tf_op jit(solution)/shard_map/psum | solution.py:14
  84.8 1.0 multiply_reduce_fusion.3
  85.8 3.6 select_convert_fusion
  89.5 29.3 %while.14 = (s32[]{:T(128)}, f32[4,512,512]{2,1,0:T(8,128)}, f32[4,512]{1,0:T(4,128)S(1)}, f32[]{:T(128)}, f32[]{:T(128)}, /*index=5*/bf16[4,512,128]{2,1,0:T(8,...) while((s32[]{:T(128)}, f32[4,512,512]{2,1,0:T(8,128)}, ...), condition=%wide.region_9.10_spmd, body=%wide.region_6.9_spmd.sunk | while | flops 1351546368 | bytes 19178136 | solution.py:92
  89.5 1.2 multiply_reduce_fusion.9
  91.0 2.8 exponential_convert_fusion.2
  93.8 2.3 fusion.147
  96.8 1.2 multiply_reduce_fusion.9
  98.3 2.8 exponential_convert_fusion.2
  101.1 2.3 fusion.147
  104.1 1.2 multiply_reduce_fusion.9
  105.7 2.8 exponential_convert_fusion.2
  108.5 2.3 fusion.147
  111.5 1.2 multiply_reduce_fusion.9
  113.0 2.8 exponential_convert_fusion.2
  115.8 2.3 fusion.147
  119.5 0.8 multiply_reduce_fusion.5
  120.4 118.6 %all-reduce.8.cloned.1.call-done = f32[2048,512]{1,0:T(8,128)} async-done(((f32[2048,512]{1,0:T(8,128)}), f32[2048,512]{1,0:T(8,128)}) %all-reduce.8.cloned.1.call-update) | async-done | bytes 4194320 | tf_op jit(solution)/shard_map/psum | solution.py:95
  239.0 1.8 fusion.7
  240.8 52.2 %all-gather.2.cloned.1.call-done = f32[2048,512]{1,0:T(8,128)} async-done(((f32[64,512]{1,0:T(8,128)}), f32[2048,512]{1,0:T(8,128)}) %all-gather.2.cloned.1.call-update) | async-done | bytes 4194320 | tf_op jit(solution)/shard_map/all_gather | solution.py:109
  293.0 2.3 slice.154
  295.3 1.6 copy.53
  296.8 1.1 broadcast_select_fusion
  299.8 66.2 %psum.38 = f32[2048]{0:T(1024)S(1)} all-reduce(f32[2048]{0:T(1024)S(1)} %bitcast.157), channel_id=1, replica_groups=mesh['dp'=32,'ind'=8] {'dp'}, use_global_device_ids=true, to_apply=%region_20.21 | all-reduce | flops 2048 | bytes 16384 | tf_op jit(solution)/shard_map/psum | solution.py:95
  366.7 63.7 %all-reduce.1 = f32[2048]{0:T(1024)S(1)} all-reduce(f32[2048]{0:T(1024)S(1)} %fusion.106), channel_id=1, replica_groups=mesh['dp'=32,'ind'=8] {'dp'}, use_global_device_ids=true, to_apply=%add.1 | all-reduce | flops 2048 | bytes 16384
  430.4 17.9 %psum.39 = f32[512]{0:T(512)S(1)} all-reduce(f32[512]{0:T(512)S(1)} %slice_select_fusion.1), channel_id=1, replica_groups=mesh['dp'=32,'ind'=8] {'ind'}, use_global_device_ids=true, to_apply=%region_21.22 | all-reduce | flops 512 | bytes 4096 | tf_op jit(solution)/shard_map/psum | solution.py:14
  448.4 1.6 copy.41
  449.9 1.5 fusion.31
  451.4 1.0 copy-done.2
  452.4 11.7 %cholesky.103 = f32[128,128]{1,0:T(8,128)S(1)} custom-call(f32[128,128]{1,0:T(8,128)S(1)} %cholesky.263), custom_call_target="Cholesky" | custom-call | tf_op jit(solution)/shard_map/jit(cholesky)/cholesky | solution.py:116
  464.2 9.8 %custom-call.32 = f32[1,128,128]{1,2,0:T(8,128)S(1)} custom-call(f32[1,128,128]{2,1,0:T(8,128)S(1)} %get-tuple-element.182), custom_call_target="InvertDiagBlocksLowerTriangular" | custom-call | tf_op jit(solution)/shard_map/jit(cholesky)/cholesky | solution.py:116
  474.0 1.2 fusion.50
  475.2 1.3 convolution_subtract_fusion
  476.5 11.7 %cholesky.215 = f32[128,128]{1,0:T(8,128)S(1)} custom-call(f32[128,128]{1,0:T(8,128)S(1)} %cholesky.267), custom_call_target="Cholesky" | custom-call | tf_op jit(solution)/shard_map/jit(cholesky)/cholesky | solution.py:116
  490.4 1.0 cholesky.222
  491.4 11.4 %custom-call.33 = f32[1,128,128]{1,2,0:T(8,128)} custom-call(f32[1,128,128]{2,1,0:T(8,128)} %get-tuple-element.180), custom_call_target="InvertDiagBlocksLowerTriangular" | custom-call | tf_op jit(solution)/shard_map/jit(cholesky)/cholesky | solution.py:116
  502.8 0.8 constant_dynamic-update-slice_fusion.2
  503.7 1.2 convolution_dynamic-update-slice_fusion
  504.8 1.5 convolution_subtract_fusion.1
  506.4 11.7 %cholesky.236 = f32[128,128]{1,0:T(8,128)S(1)} custom-call(f32[128,128]{1,0:T(8,128)S(1)} %cholesky.272), custom_call_target="Cholesky" | custom-call | tf_op jit(solution)/shard_map/jit(cholesky)/cholesky | solution.py:116
  518.1 1.1 select_reduce_fusion.1
  519.3 10.6 %custom-call.34 = f32[1,128,128]{1,2,0:T(8,128)S(1)} custom-call(f32[1,128,128]{2,1,0:T(8,128)} %get-tuple-element.178), custom_call_target="InvertDiagBlocksLowerTriangular" | custom-call | tf_op jit(solution)/shard_map/jit(cholesky)/cholesky | solution.py:116
  530.3 1.3 convolution_subtract_fusion.2
  531.6 11.9 %cholesky.253 = f32[128,128]{1,0:T(8,128)S(1)} custom-call(f32[128,128]{1,0:T(8,128)S(1)} %convolution_subtract_fusion.2), custom_call_target="Cholesky" | custom-call | tf_op jit(solution)/shard_map/jit(cholesky)/cholesky | solution.py:116
  543.7 1.4 compare_reduce_fusion.1
  549.0 2.4 fusion.32
  552.0 14.4 %while.15 = (s32[]{:T(128)}, f32[512,512]{0,1:T(8,128)}, s32[4,2]{0,1:T(2,128)S(1)}, f32[4,128,128]{2,1,0:T(8,128)}, s32[]{:T(128)}) while((s32[]{:T(128)}, f32[512,512]{0,1:T(8,128)}, s32[4,2]{0,1:T(2,128)S(1)}, f32[4,128,128]{2,1,0:T(8,128)}, s32[]{:T(128)}) %tuple.55), condition=%wide.while_cond, body=%wide.while_body.sunk | while | flops 2 | bytes 393829 | solution.py:121
  552.6 2.3 dynamic-slice.8
  556.2 2.3 dynamic-slice.8
  559.8 2.3 dynamic-slice.8
  563.4 2.2 dynamic-slice.8
  566.4 40.1 %custom-call.35 = f32[4,128,128]{1,2,0:T(8,128)S(1)} custom-call(f32[4,128,128]{2,1,0:T(8,128)} %get-tuple-element.102), custom_call_target="InvertDiagBlocksLowerTriangular" | custom-call | tf_op jit(solution)/shard_map/triangular_solve | solution.py:121
  606.9 1.0 fusion.10
  608.0 1.1 fusion.11
  609.3 1.2 fusion.14
  611.3 1.0 convolution_subtract_fusion.5
  612.5 1.1 convolution_subtract_fusion.4
  613.8 1.2 convolution_subtract_fusion.3
  615.2 4.5 gather_fusion
  620.5 1.4 fusion.12
  (119 shorter events, 21.4 us)
Async XLA Ops:
  7.2 3.3 copy-start
  7.2 77.6 %all-reduce.6.cloned.1.call-start = ((), (), s32[]{:S(2)}) async-start(), calls=%async_computation | async-start | bytes 262144 | tf_op jit(solution)/shard_map/psum | solution.py:14
  9.0 230.0 %all-reduce.8.cloned.1.call-start = ((), (), s32[]{:S(2)}) async-start(), calls=%async_computation.1 | async-start | bytes 8388608 | tf_op jit(solution)/shard_map/psum | solution.py:95
  10.5 2.1 copy-start.9
  10.5 30.5 %copy-start.10 = (s32[32]{0:T(128)S(1)}, s32[32]{0:T(128)}, u32[]{:S(2)}) copy-start(s32[32]{0:T(128)} %param.15) | copy-start | bytes 388
  10.5 32.7 %copy-start.8 = (bf16[2048]{0:T(1024)(128)(2,1)S(1)}, bf16[2048]{0:T(1024)(128)(2,1)}, u32[]{:S(2)}) copy-start(bf16[2048]{0:T(1024)(128)(2,1)} %param.14) | copy-start | bytes 12292
  89.5 4.3 copy-start.11
  96.8 4.3 copy-start.11
  104.1 4.3 copy-start.11
  111.5 4.3 copy-start.11
  118.8 120.2 %copy-start.5 = (bf16[512,128]{1,0:T(8,128)(2,1)S(1)}, bf16[512,128]{1,0:T(8,128)(2,1)}, u32[]{:S(2)}) copy-start(bf16[512,128]{1,0:T(8,128)(2,1)} %all-reduce.6.cloned.1.call-done) | copy-start | bytes 393220
  118.8 174.2 %all-gather.2.cloned.1.call-start = ((), (), s32[]{:S(2)}) async-start(), calls=%async_computation.2 | async-start | bytes 4325376 | tf_op jit(solution)/shard_map/all_gather | solution.py:109
  239.0 59.0 %copy-start.12 = (u32[256]{0:T(256)S(1)}, u32[256]{0:T(256)}, u32[]{:S(2)}) copy-start(u32[256]{0:T(256)} %constant.249) | copy-start | bytes 3076
  240.8 207.6 %all-reduce.10.cloned.1.call-start = ((), (), s32[]{:S(2)}) async-start(), calls=%async_computation.3 | async-start | bytes 2097152 | tf_op jit(solution)/shard_map/psum | solution.py:14
  366.0 0.6 copy-start.6
  451.4 1.0 copy-start.2
  504.8 101.7 %copy-start.4 = (f32[64,512]{1,0:T(8,128)S(1)}, f32[64,512]{1,0:T(8,128)}, u32[]{:S(2)}) copy-start(f32[64,512]{1,0:T(8,128)} %fusion.7) | copy-start | bytes 393220
  545.7 2.7 copy-start.1
  609.3 2.0 copy-start.7
  615.2 7.4 %copy-start.3 = (f32[64,512]{1,0:T(8,128)}, f32[64,512]{1,0:T(8,128)S(1)}, u32[]{:S(2)}) copy-start(f32[64,512]{1,0:T(8,128)S(1)} %pad_maximum_fusion) | copy-start | bytes 393220
Sparse Core Ops, SparseCore 0:
  10.9 73.8 all-reduce.5
  118.9 119.9 all-reduce.7
  242.1 50.8 all-gather.1
  298.1 75.4 all-reduce.9
where the time goes:
time: 638 us; the launch traced here: 630 us
  waiting for transfers between devices  212 us (33%)
  blocking collectives  175 us (27%)
  other arithmetic  143 us (22%)
  matrix products  47.9 us (8%)
  local copies, waits for them, and re-layouts  31.2 us (5%)
  between operations  21.6 us (3%)
    psum x1, waiting for transfers between devices, body(): gram_total, cross_total = lax.psum((gram_rows, cross_rows), 'dp')  119 us
    another operation x14, other arithmetic, body(): factor_top = jnp.linalg.cholesky(system_top)  83.5 us
    psum x1, blocking collectives, body(): gram_total, cross_total = lax.psum((gram_rows, cross_rows), 'dp')  66.2 us
    unnamed x1, blocking collectives  63.7 us
    all_gather x1, waiting for transfers between devices, body(): lax.all_gather(system_rows, 'dp', axis=0, tiled=True)  52.2 us
    another operation x4, other arithmetic, body(): lax.linalg.triangular_solve(factor_top, system_rows, left_side=False, low...  43 us
    psum x2, waiting for transfers between devices, from_root(): return lax.psum(jnp.where(mine, shard, jnp.zeros_like(shard)), axis)  40.8 us
    all_gather x1, blocking collectives, body(): embedded = lax.all_gather(embedded_piece, 'ind', axis=0, tiled=True)  27.6 us
  transfers between devices with their start and end apart: 4, of which 3 were waited for; matrix products, arithmetic and copies ran while one was open for 1% of the time, Pallas kernels for 0%

commit v1 on v0

v1 whole, which is shorter than its diff:
```python
import functools
import jax
import jax.numpy as jnp
from jax import lax
from jax.experimental import pallas as pl
from jax.experimental.pallas import tpu as pltpu
from jax.sharding import PartitionSpec as P

PB = 512
JITTER = 0.0001
LOG2E = 1.4426950408889634
LN2 = 0.6931471805599453
MASKED = -1.0e6
F32, BF16 = jnp.float32, jnp.bfloat16
HI = lax.Precision.HIGHEST
NT = (((1,), (1,)), ((), ()))
TN = (((0,), (0,)), ((), ()))


def vmem(limit=60 << 20):
    return pltpu.CompilerParams(vmem_limit_bytes=limit)


def widen(points, half, first):
    rows = points.shape[0]
    high = half.astype(BF16)
    rest = half - high.astype(F32)
    mid = rest.astype(BF16)
    low = (rest - mid.astype(F32)).astype(BF16)
    lane = lax.broadcasted_iota(jnp.int32, (rows, 128), 1)
    at = 0 if first else 3
    one = 3 if first else 0
    tail = jnp.where((lane >= one) & (lane < one + 3), 1.0, 0.0)
    tail = jnp.where(lane == at, high.astype(F32), tail)
    tail = jnp.where(lane == at + 1, mid.astype(F32), tail)
    tail = jnp.where(lane == at + 2, low.astype(F32), tail)
    return jnp.concatenate([points, tail.astype(BF16)], axis=1)


def half_norm(points):
    wide = points.astype(F32)
    return -0.5 * jnp.sum(wide * wide, axis=1, keepdims=True)


def gelu(x):
    inner = x * (0.7978845608028654 + 0.035677408136300125 * (x * x))
    half = 0.5 * x
    return half + half * jnp.tanh(inner)


def embed_kernel(count_ref, x_ref, w1_ref, w2_ref, w3_ref, gain_ref, out_ref):
    rows = x_ref.shape[0]
    one = gelu(jnp.dot(x_ref[...], w1_ref[...], preferred_element_type=F32)).astype(BF16)
    two = gelu(jnp.dot(one, w2_ref[...], preferred_element_type=F32)).astype(BF16)
    proj = jnp.dot(two, w3_ref[...], preferred_element_type=F32)
    mean = jnp.mean(proj * proj, axis=1, keepdims=True)
    points = (proj * lax.rsqrt(mean + 1e-06) * gain_ref[...]).astype(BF16)
    index = pl.program_id(0) * rows + lax.broadcasted_iota(jnp.int32, (rows, 1), 0)
    half = jnp.where(index < count_ref[0], half_norm(points), MASKED)
    out_ref[...] = widen(points, half, False)


def embed(count, inputs, w_in, w_mid, w_out, gain, tile=512):
    slots = inputs.shape[0]
    whole = lambda a: pl.BlockSpec(a.shape, lambda i: (0, 0), pipeline_mode=pl.Buffered(1))
    return pl.pallas_call(
        embed_kernel,
        out_shape=jax.ShapeDtypeStruct((slots, 256), BF16),
        grid=(slots // tile,),
        in_specs=[
            pl.BlockSpec(memory_space=pltpu.SMEM),
            pl.BlockSpec((tile, inputs.shape[1]), lambda i: (i, 0)),
            whole(w_in),
            whole(w_mid),
            whole(w_out),
            whole(gain),
        ],
        out_specs=pl.BlockSpec((tile, 256), lambda i: (i, 0)),
        compiler_params=vmem(),
        cost_estimate=pl.CostEstimate(flops=6 * 10**9, bytes_accessed=5 << 20, transcendentals=4 << 20),
        name="embed",
    )(count, inputs, w_in, w_mid, w_out, gain)


def panel_kernel(scale_ref, samples_ref, panel_ref, chunk_ref, tcol_ref, trow_ref, pt_ref, top_ref):
    step = pl.program_id(0)
    i2, offset = scale_ref[0], scale_ref[1]
    samples = samples_ref[...]
    panel = widen(panel_ref[...], half_norm(panel_ref[...]) + offset, True)
    chunk = widen(chunk_ref[...], half_norm(chunk_ref[...]) + offset, True)
    kern = jnp.exp2(i2 * lax.dot_general(samples, panel, NT, preferred_element_type=F32)).astype(BF16)
    part = jnp.exp2(i2 * lax.dot_general(chunk, samples, NT, preferred_element_type=F32)).astype(BF16)
    left = jnp.concatenate([part, trow_ref[...]], axis=0)
    lane = lax.broadcasted_iota(jnp.int32, (samples.shape[0], 128), 1)
    column = jnp.where(lane == 0, tcol_ref[...].astype(F32), 0.0).astype(BF16)
    pt_ref[:, :PB] = kern
    pt_ref[:, PB:] = column
    sums = jnp.dot(left, kern, preferred_element_type=F32)

    @pl.when(step == 0)
    def _():
        top_ref[...] = sums

    @pl.when(step > 0)
    def _():
        top_ref[...] += sums


def panel_top(scales, samples, panel, chunk, tcol, trow, tile=512):
    slots = samples.shape[0]
    rows = chunk.shape[0] + trow.shape[0]
    fixed = lambda a: pl.BlockSpec(a.shape, lambda i: (0, 0))
    return pl.pallas_call(
        panel_kernel,
        out_shape=(jax.ShapeDtypeStruct((slots, PB + 128), BF16), jax.ShapeDtypeStruct((rows, PB), F32)),
        grid=(slots // tile,),
        in_specs=[
            pl.BlockSpec(memory_space=pltpu.SMEM),
            pl.BlockSpec((tile, 256), lambda i: (i, 0)),
            fixed(panel),
            fixed(chunk),
            pl.BlockSpec((tile, 1), lambda i: (i, 0)),
            pl.BlockSpec((trow.shape[0], tile), lambda i: (0, i)),
        ],
        out_specs=(pl.BlockSpec((tile, PB + 128), lambda i: (i, 0)), pl.BlockSpec((rows, PB), lambda i: (0, 0))),
        compiler_params=vmem(),
        cost_estimate=pl.CostEstimate(flops=10**9, bytes_accessed=5 << 20, transcendentals=1 << 20),
        name="panel",
    )(scales, samples, panel, chunk, tcol, trow)


def gram_kernel(scale_ref, points_ref, samples_ref, pt_ref, out_ref):
    i2, offset = scale_ref[0], scale_ref[1]
    rows = points_ref.shape[0]
    points = widen(points_ref[...], half_norm(points_ref[...]) + offset, True)
    kern = jnp.exp2(
        i2 * lax.dot_general(points, samples_ref[...], NT, preferred_element_type=F32)
    ).astype(BF16)
    sums = jnp.dot(kern, pt_ref[...], preferred_element_type=F32)
    crossed = sums[:, PB:].T
    for b in range(rows // 64):
        out_ref[b, :64, :] = sums[b * 64 : b * 64 + 64, :PB]
        out_ref[b, 64:, :] = jnp.concatenate(
            [crossed[:8, b * 64 : b * 64 + 64], jnp.zeros((8, PB - 64), F32)], axis=1
        )


def gram(scales, points, samples, pt, tile=256):
    total = points.shape[0]
    whole = lambda a: pl.BlockSpec(a.shape, lambda i: (0, 0), pipeline_mode=pl.Buffered(1))
    return pl.pallas_call(
        gram_kernel,
        out_shape=jax.ShapeDtypeStruct((total // 64, 72, PB), F32),
        grid=(total // tile,),
        in_specs=[
            pl.BlockSpec(memory_space=pltpu.SMEM),
            pl.BlockSpec((tile, 128), lambda i: (i, 0)),
            whole(samples),
            whole(pt),
        ],
        out_specs=pl.BlockSpec((tile // 64, 72, PB), lambda i: (i, 0, 0)),
        compiler_params=vmem(),
        cost_estimate=pl.CostEstimate(flops=8 * 10**9, bytes_accessed=9 << 20, transcendentals=4 << 20),
        name="gram",
    )(scales, points, samples, pt)


def invert_block(block, store, note):
    groups = [block[8 * v : 8 * v + 8, :] for v in range(16)]
    lane = lax.broadcasted_iota(jnp.int32, (8, 128), 1)
    pivots = jnp.ones((8, 128), F32)
    spread = lambda a: jnp.broadcast_to(a, (8, 128))
    for g in range(32):
        j = 4 * g
        v, s = j // 8, j % 8
        inside = (lane >= j) & (lane < j + 4)
        raw = [spread(groups[v][s + a : s + a + 1, :]) for a in range(4)]
        p = [[spread(raw[a][:, j + b : j + b + 1]) for b in range(a + 1)] for a in range(4)]
        live = [u for u in range(v, 16) if not (u == v and s == 4)]
        cols = {u: [spread(groups[u][:, j + b : j + b + 1]) for b in range(4)] for u in live}
        d0 = p[0][0]
        i0 = 1.0 / d0
        l10, l20, l30 = p[1][0] * i0, p[2][0] * i0, p[3][0] * i0
        d1 = p[1][1] - l10 * p[1][0]
        i1 = 1.0 / d1
        q21, q31 = p[2][1] - l20 * p[1][0], p[3][1] - l30 * p[1][0]
        l21, l31 = q21 * i1, q31 * i1
        d2 = p[2][2] - l20 * p[2][0] - l21 * q21
        i2 = 1.0 / d2
        q32 = p[3][2] - l30 * p[2][0] - l31 * q21
        l32 = q32 * i2
        d3 = p[3][3] - l30 * p[3][0] - l31 * q31 - l32 * q32
        i3 = 1.0 / d3
        r = [
            jnp.where(inside, jnp.where(lane == j + a, 1.0, 0.0), raw[a]) for a in range(4)
        ]
        r[1] = r[1] - l10 * r[0]
        r[2] = r[2] - l20 * r[0] - l21 * r[1]
        r[3] = r[3] - l30 * r[0] - l31 * r[1] - l32 * r[2]
        for a, d in enumerate((d0, d1, d2, d3)):
            store(j + a, r[a] * lax.rsqrt(d))
            pivots = jnp.where(lane == j + a, d, pivots)
        q3 = r[3] * i3
        q2 = r[2] * i2 - l32 * q3
        q1 = r[1] * i1 - l21 * q2 - l31 * q3
        q0 = r[0] * i0 - l10 * q1 - l20 * q2 - l30 * q3
        for u in live:
            c = cols[u]
            base = jnp.where(inside, 0.0, groups[u])
            groups[u] = base - (c[0] * q0 + c[1] * q1) - (c[2] * q2 + c[3] * q3)
    return pivots


def factor_kernel(scale_ref, panel_ref, top_ref, inverse_ref, log_ref, work, piece):
    i2, offset, over, jit = scale_ref[0], scale_ref[1], scale_ref[2], scale_ref[3]
    half = half_norm(panel_ref[...])
    left = widen(panel_ref[...], half + offset, True)
    right = widen(panel_ref[...], half, False)
    kern = jnp.exp2(i2 * lax.dot_general(left, right, NT, preferred_element_type=F32))
    row = lax.broadcasted_iota(jnp.int32, (PB, PB), 0)
    col = lax.broadcasted_iota(jnp.int32, (PB, PB), 1)
    work[...] = kern + jnp.where(row == col, jit, 0.0) + top_ref[...] * over
    total = jnp.zeros((8, 128), F32)
    lane = lax.broadcasted_iota(jnp.int32, (128, 128), 1)

    def store(r, line):
        piece[r : r + 1, :] = line[:1, :]

    for k in range(PB // 128):
        lo, hi = 128 * k, 128 * k + 128
        lower = lax.broadcasted_iota(jnp.int32, (128, 128), 0) >= lane
        pivots = invert_block(work[lo:hi, lo:hi], store, None)
        total = total + jnp.log(pivots)
        t = jnp.where(lower, piece[...], 0.0)
        rest = jnp.dot(t, work[lo:hi, :], preferred_element_type=F32, precision=HI)
        parts = [rest[:, :lo]] * (lo > 0) + [t] + [rest[:, hi:]] * (hi < PB)
        u = jnp.concatenate(parts, axis=1)
        inverse_ref[lo:hi, :] = jnp.where(
            lax.broadcasted_iota(jnp.int32, (128, PB), 1) < hi, u, 0.0
        )
        if hi < PB:
            away = lax.dot_general(u[:, hi:], u, TN, preferred_element_type=F32, precision=HI)
            column = lax.broadcasted_iota(jnp.int32, (PB - hi, PB), 1)
            kept = jnp.where((column >= lo) & (column < hi), 0.0, work[hi:, :])
            work[hi:, :] = kept - away
    log_ref[...] = jnp.broadcast_to(jnp.sum(total[:1, :], axis=1, keepdims=True), (8, 128))


def factor(scales, panel, top):
    return pl.pallas_call(
        factor_kernel,
        out_shape=(jax.ShapeDtypeStruct((PB, PB), F32), jax.ShapeDtypeStruct((8, 128), F32)),
        in_specs=[
            pl.BlockSpec(memory_space=pltpu.SMEM),
            pl.BlockSpec(memory_space=pltpu.VMEM),
            pl.BlockSpec(memory_space=pltpu.VMEM),
        ],
        out_specs=(pl.BlockSpec(memory_space=pltpu.VMEM), pl.BlockSpec(memory_space=pltpu.VMEM)),
        scratch_shapes=[pltpu.VMEM((PB, PB), F32), pltpu.VMEM((128, 128), F32)],
        compiler_params=vmem(),
        cost_estimate=pl.CostEstimate(flops=20 * 10**9, bytes_accessed=4 << 20, transcendentals=1 << 20),
        name="factor",
    )(scales, panel, top)


def finish_kernel(place_ref, scale_ref, own_ref, panel_ref, sums_ref, right_ref, inverse_ref, pf_ref, rhs_ref, sol_ref):
    i2, offset, over, jit = scale_ref[0], scale_ref[1], scale_ref[2], scale_ref[3]
    rows = own_ref.shape[0]
    left = widen(own_ref[...], half_norm(own_ref[...]) + offset, True)
    right = widen(panel_ref[...], half_norm(panel_ref[...]), False)
    kern = jnp.exp2(i2 * lax.dot_general(left, right, NT, preferred_element_type=F32))
    row = place_ref[0] + lax.broadcasted_iota(jnp.int32, (rows, PB), 0)
    col = lax.broadcasted_iota(jnp.int32, (rows, PB), 1)
    system = kern + jnp.where(row == col, jit, 0.0) + sums_ref[:rows, :] * over
    both = jnp.concatenate([system, right_ref[...] * over], axis=0)
    solved = lax.dot_general(both, inverse_ref[...], NT, preferred_element_type=F32, precision=HI)
    pf = solved[:rows, :]
    sol = solved[rows:, :]
    pf_ref[...] = pf
    sol_ref[...] = sol
    back = lax.dot_general(sol, pf, NT, preferred_element_type=F32, precision=HI)
    rhs_ref[...] = sums_ref[rows:, :rows] * over - back


def finish(place, scales, own, panel, sums, right, inverse):
    rows = own.shape[0]
    smem = pl.BlockSpec(memory_space=pltpu.SMEM)
    full = pl.BlockSpec(memory_space=pltpu.VMEM)
    return pl.pallas_call(
        finish_kernel,
        out_shape=(
            jax.ShapeDtypeStruct((rows, PB), F32),
            jax.ShapeDtypeStruct((8, rows), F32),
            jax.ShapeDtypeStruct((8, PB), F32),
        ),
        in_specs=[smem, smem] + [full] * 5,
        out_specs=(full, full, full),
        compiler_params=vmem(),
        cost_estimate=pl.CostEstimate(flops=10**9, bytes_accessed=2 << 20, transcendentals=1 << 16),
        name="finish",
    )(place, scales, own, panel, sums, right, inverse)


SHARDS, LAYERS = 32, 8


def moved(x, axis, size, to):
    return lax.ppermute(x, axis, [(i, to(i)) for i in range(size)])


def along_x(i, k):
    return (i // 8) * 8 + (i + 2 * k) % 8


def along_y(i, k):
    return (i + 8 * k) % SHARDS


def sum_over(x, step):
    return x + sum(moved(x, "dp", SHARDS, functools.partial(step, k=k)) for k in (1, 2, 3))


def top_everywhere(top, core):
    rows = top.shape[1]
    kept = lax.dynamic_index_in_dim(top, core, 0, False)
    sent = lax.dynamic_index_in_dim(top, 1 - core, 0, False)
    half = kept + moved(sent, "dp", SHARDS, lambda i: i ^ 1)
    half = sum_over(half, along_x)
    half = sum_over(half, along_y)
    layer = lax.axis_index("ind")
    parts = jnp.zeros((LAYERS, rows, 256), F32)
    ahead = behind = half
    parts = lax.dynamic_update_index_in_dim(parts, half, layer, 0)
    for k in range(1, 5):
        ahead = moved(ahead, "ind", LAYERS, lambda i: (i + 1) % LAYERS)
        parts = lax.dynamic_update_index_in_dim(parts, ahead, (layer - k) % LAYERS, 0)
        if k < 4:
            behind = moved(behind, "ind", LAYERS, lambda i: (i - 1) % LAYERS)
            parts = lax.dynamic_update_index_in_dim(parts, behind, (layer + k) % LAYERS, 0)
    other = moved(parts, "dp", SHARDS, lambda i: i ^ 1)
    left = jnp.where(core == 0, parts, other)
    right = jnp.where(core == 0, other, parts)
    return jnp.concatenate([left, right], axis=2)


def body(
    inputs, targets, row_counts, w_in, w_mid, w_out, feat_gain, inducing, log_scale, lengthscale, noise_var
):
    shard = lax.axis_index("dp")
    layer = lax.axis_index("ind")
    core = shard % 2
    slots = inputs.shape[0]
    inv_sq = 1.0 / (lengthscale[0] * lengthscale[0])
    scales = jnp.stack(
        [inv_sq * LOG2E, log_scale[0] / inv_sq, 1.0 / noise_var[0], jnp.asarray(JITTER, F32)]
    )
    first = inducing[:PB]
    panel = first
    for k in range(1, LAYERS):
        got = lax.ppermute(first, "ind", [(0, k)])
        panel = jnp.where(layer == k, got, panel)
    count = lax.dynamic_slice_in_dim(row_counts, shard, 1, 0)
    samples = embed(count, inputs, w_in, w_mid, w_out, feat_gain.reshape(1, -1))
    chunk = lax.dynamic_slice_in_dim(panel, layer * 64, 64, 0)
    trow = jnp.broadcast_to(targets.reshape(1, slots), (8, slots))
    pt, top = panel_top(scales, samples, panel, chunk, targets.reshape(slots, 1), trow)
    rows = top.shape[0]
    whole = top_everywhere(jnp.stack([top[:, :256], top[:, 256:]]), core)
    sums = gram(scales, inducing, samples, pt)
    own = lax.psum_scatter(sums, "dp", scatter_dimension=0, tiled=True)[0]
    system_top = whole[:, :64].reshape(PB, PB)
    right_top = whole[0, 64:]
    inverse, logs = factor(scales, panel, system_top)
    own_rows = inducing.shape[0] // SHARDS
    points = lax.dynamic_slice_in_dim(inducing, shard * own_rows, own_rows, 0)
    place = (layer * inducing.shape[0] + shard * own_rows).reshape(1).astype(jnp.int32)
    pf, rhs, sol = finish(place, scales, points, panel, own, right_top, inverse)
    return pf, rhs[0], sol[0], logs[0, :1]


def solution(mesh):
    return jax.shard_map(
        body,
        mesh=mesh,
        in_specs=(P("dp", None), P("dp"), P(), P(), P(), P(), P(), P("ind", None), P(), P(), P()),
        out_specs=(P(("ind", "dp"), None), P(("ind", "dp")), P(), P()),
        check_vma=False,
    )
```

time: 638 us -> 167 us (0.26)
  waiting for transfers between devices: 212 us -> 31.1 us
  blocking collectives: 175 us -> 0 us
  other arithmetic: 143 us -> 3.49 us
  Pallas kernels: 0 us -> 68.4 us
  matrix products: 47.9 us -> 0 us
  starting transfers between devices: 0.16 us -> 34.7 us
  local copies, waits for them, and re-layouts: 31.2 us -> 10.6 us
    psum x3 -> x0, waiting for transfers between devices: 159 us -> none  [the longest x1 119 us: body(): gram_total, cross_total = lax.psum((gram_rows, cross_rows), 'dp')]
    another operation x19 -> x1, other arithmetic: 127 us -> 0.59 us  [body(): jnp.stack([inv_sq * LOG2E, log_scale[0] / inv_sq, 1.0 / noise_var[0], jnp...]
    psum x2 -> x0, blocking collectives: 84.1 us -> none  [the longest x1 66.2 us: body(): gram_total, cross_total = lax.psum((gram_rows, cross_rows), 'dp')]
    pallas_call x0 -> x5, Pallas kernels: none -> 68.4 us  [the longest x1 32.9 us: factor(): pl.pallas_call(factor_kernel, out_shape=(jax.ShapeDtypeStruct((PB, PB), F...]
    unnamed x1 -> x0, blocking collectives: 63.7 us -> none
    all_gather x1 -> x0, waiting for transfers between devices: 52.2 us -> none  [body(): lax.all_gather(system_rows, 'dp', axis=0, tiled=True)]
    ppermute x0 -> x22, starting transfers between devices: none -> 34.6 us  [the longest x15 20.8 us: moved(): return lax.ppermute(x, axis, [(i, to(i)) for i in range(size)])]
    dot_general x17 -> x0, matrix products: 33.1 us -> none  [the longest x6 16.4 us: exponent(): cross_term = jnp.dot(points, others.T, preferred_element_type=jnp.float32)]
  transfers between devices with their start and end apart: 4 -> 23, of which waited for: 3 -> 9; matrix products, arithmetic and copies ran while one was open for 1% -> 5% of each run, Pallas kernels for 0% -> 27%
where the time goes in v1:
time: 167 us; the launch traced here: 165 us
  Pallas kernels  68.4 us (41%)
  starting transfers between devices  34.7 us (21%)
  waiting for transfers between devices  31.1 us (19%)
  between operations  16.4 us (10%)
  local copies, waits for them, and re-layouts  10.6 us (6%)
  other arithmetic  3.49 us (2%)
    pallas_call x1, Pallas kernels, factor(): pl.pallas_call(factor_kernel, out_shape=(jax.ShapeDtypeStruct((PB, PB), F...  32.9 us
    ppermute x15, waiting for transfers between devices, moved(): return lax.ppermute(x, axis, [(i, to(i)) for i in range(size)])  23.3 us
    ppermute x15, starting transfers between devices, moved(): return lax.ppermute(x, axis, [(i, to(i)) for i in range(size)])  20.8 us
    pallas_call x1, Pallas kernels, gram(): pl.pallas_call(gram_kernel, out_shape=jax.ShapeDtypeStruct((total // 64,...  14.4 us
    ppermute x7, starting transfers between devices, body(): got = lax.ppermute(first, 'ind', [(0, k)])  13.8 us
    pallas_call x1, Pallas kernels, embed(): pl.pallas_call(embed_kernel, out_shape=jax.ShapeDtypeStruct((slots, 256),...  12.2 us
    reduce_scatter x1, waiting for transfers between devices, body(): own = lax.psum_scatter(sums, 'dp', scatter_dimension=0, tiled=True)[0]  7.76 us
    pallas_call x1, Pallas kernels, panel_top(): pl.pallas_call(panel_kernel, out_shape=(jax.ShapeDtypeStruct((slots, PB +...  5.31 us
  transfers between devices with their start and end apart: 23, of which 9 were waited for; matrix products, arithmetic and copies ran while one was open for 5% of the time, Pallas kernels for 27%

profile of v1, /device:TPU:0, one launch (start us, length us, event | category | flops | bytes accessed | tf_op | source)
XLA Modules:
  0.0 164.7 jit_solution(3721239666542000032)
XLA Ops:
  7.2 0.0 reduce-scatter.2.cloned.1.call-start
  7.2 0.9 slice.24
  8.1 6.1 %collective-permute-start = (bf16[512,128]{1,0:T(8,128)(2,1)S(1)}, bf16[512,128]{1,0:T(8,128)(2,1)S(1)}, u32[]{:S(2)}, u32[]{:S(2)}) collective-permute-start(bf16[512,128]{1,0:T(8,128)(2,1)S(1)} %slice.24), channel_id=1, source_target_pairs={{0,7},{8,15},{16,23},{24,31},{32,39},{40,47},{48,55},{56,63},{64,7... | collective-permute-start | bytes 393224 | tf_op jit(solution)/shard_map/ppermute | solution.py:360
  14.2 1.3 collective-permute-start.1
  15.5 1.3 collective-permute-start.2
  16.8 1.3 collective-permute-start.3
  18.1 1.3 collective-permute-start.4
  19.4 1.2 dynamic_slice.17.count_ref
  20.7 0.0 collective-permute-done
  20.7 1.3 collective-permute-start.5
  22.0 0.0 collective-permute-done.1
  22.0 1.3 collective-permute-start.6
  23.3 0.0 copy-start.2
  23.3 12.2 %embed.1.samples_ref = bf16[2048,256]{1,0:T(8,128)(2,1)} custom-call(s32[1]{0:T(128)} %dynamic_slice.17.count_ref, bf16[2048,256]{1,0:T(8,128)(2,1)} %x_ref.1, bf16[256,1024]{1,0:T(8,128)(2,1)} %w1_ref.1, bf16[1024,1024]{1,0:T(8,128)(2,1)} %w2_ref.1, bf16[1024,128]{1,0:T(8,128)(2,1)} %w3_ref.1, f32[1,128]{1,0:T(1,128)} %bitcast.39), custom_call_target="tpu_custom_call" | custom-call | flops 6000000000 | bytes 5242880 | tf_op jit(solution)/shard_map/embed/pallas_call | solution.py:66
  37.5 1.1 reshape.37.tcol_ref
  38.7 0.6 pad_maximum_fusion.1.scale_ref
  39.3 0.0 collective-permute-done.2
  39.3 0.0 collective-permute-done.3
  39.3 0.0 collective-permute-done.4
  39.3 0.0 collective-permute-done.5
  39.3 0.0 collective-permute-done.6
  39.3 1.0 select_select_fusion.panel_ref
  40.3 0.7 constant_dynamic-slice_fusion.chunk_ref
  40.9 0.6 broadcast_in_dim.33.trow_ref
  41.6 5.3 %panel.1 = (bf16[2048,640]{1,0:T(8,128)(2,1)}, f32[72,512]{1,0:T(8,128)}) custom-call(f32[4]{0:T(128)} %pad_maximum_fusion.1.scale_ref, bf16[2048,256]{1,0:T(8,128)(2,1)} %embed.1.samples_ref, bf16[512,128]{1,0:T(8,128)(2,1)} %copy-done, bf16[64,128]{1,0:T(8,128)(2,1)} %constant_dynamic-slice_fusion.chunk_ref, bf16[2048,1]{1,0:T(8,128)(2,1)} %reshape.37.tcol_ref, ...), custom_call_target="tpu_custom_call" | custom-call | flops 1000000000 | bytes 5242880 | tf_op jit(solution)/shard_map/panel/pallas_call | solution.py:113
  46.9 14.4 %gram.1 = f32[32,72,512]{2,1,0:T(8,128)} custom-call(f32[4]{0:T(128)} %pad_maximum_fusion.1.scale_ref, bf16[2048,128]{1,0:T(8,128)(2,1)} %points_ref.1, bf16[2048,256]{1,0:T(8,128)(2,1)} %embed.1.samples_ref, bf16[2048,640]{1,0:T(8,128)(2,1)} %get-tuple-element.11.pt_ref), custom_call_target="tpu_custom_call" | custom-call | flops 8000000000 | bytes 9437184 | tf_op jit(solution)/shard_map/gram/pallas_call | solution.py:151
  61.3 0.0 reduce-scatter.2.cloned.1.call-update
  61.3 0.9 copy-done.1
  62.2 0.1 collective-permute-start.7
  62.3 1.2 collective-permute-done.7
  63.6 2.8 %collective-permute-start.10 = (f32[72,256]{1,0:T(8,128)S(1)}, f32[72,256]{1,0:T(8,128)S(1)}, u32[]{:S(2)}, u32[]{:S(2)}) collective-permute-start(f32[72,256]{1,0:T(8,128)S(1)} %fusion.4), channel_id=1, source_target_pairs={{0,48},{8,56},{16,0},{24,8},{32,16},{40,24},{48,32},{56,40},{64,11... | collective-permute-start | bytes 221192 | tf_op jit(solution)/shard_map/ppermute | solution.py:308
  66.4 0.0 collective-permute-start.8
  66.4 2.3 %collective-permute-start.9 = (f32[72,256]{1,0:T(8,128)S(1)}, f32[72,256]{1,0:T(8,128)S(1)}, u32[]{:S(2)}, u32[]{:S(2)}) collective-permute-start(f32[72,256]{1,0:T(8,128)S(1)} %fusion.4), channel_id=1, source_target_pairs={{0,32},{8,40},{16,48},{24,56},{32,0},{40,8},{48,16},{56,24},{64,96... | collective-permute-start | bytes 221192 | tf_op jit(solution)/shard_map/ppermute | solution.py:308
  68.7 0.0 collective-permute-done.10
  68.7 4.5 %collective-permute-done.8 = f32[72,256]{1,0:T(8,128)S(1)} collective-permute-done((f32[72,256]{1,0:T(8,128)S(1)}, f32[72,256]{1,0:T(8,128)S(1)}, u32[]{:S(2)}, u32[]{:S(2)}) %collective-permute-start.8) | collective-permute-done | bytes 73760 | tf_op jit(solution)/shard_map/ppermute | solution.py:308
  73.3 0.0 collective-permute-done.9
  73.3 3.1 %collective-permute-start.13 = (f32[72,256]{1,0:T(8,128)S(1)}, f32[72,256]{1,0:T(8,128)S(1)}, u32[]{:S(2)}, u32[]{:S(2)}) collective-permute-start(f32[72,256]{1,0:T(8,128)S(1)} %add_add_fusion.1), channel_id=1, source_target_pairs={{0,192},{8,200},{16,208},{24,216},{32,224},{40,232},{48,240},{56,2... | collective-permute-start | bytes 221192 | tf_op jit(solution)/shard_map/ppermute | solution.py:308
  76.4 0.0 collective-permute-start.11
  76.4 2.2 %collective-permute-start.12 = (f32[72,256]{1,0:T(8,128)S(1)}, f32[72,256]{1,0:T(8,128)S(1)}, u32[]{:S(2)}, u32[]{:S(2)}) collective-permute-start(f32[72,256]{1,0:T(8,128)S(1)} %add_add_fusion.1), channel_id=1, source_target_pairs={{0,128},{8,136},{16,144},{24,152},{32,160},{40,168},{48,176},{56,1... | collective-permute-start | bytes 221192 | tf_op jit(solution)/shard_map/ppermute | solution.py:308
  78.6 4.1 %collective-permute-done.11 = f32[72,256]{1,0:T(8,128)S(1)} collective-permute-done((f32[72,256]{1,0:T(8,128)S(1)}, f32[72,256]{1,0:T(8,128)S(1)}, u32[]{:S(2)}, u32[]{:S(2)}) %collective-permute-start.11) | collective-permute-done | bytes 73760 | tf_op jit(solution)/shard_map/ppermute | solution.py:308
  82.7 0.0 collective-permute-done.12
  82.8 0.1 collective-permute-start.14
  82.9 3.2 %collective-permute-start.15 = (f32[72,256]{1,0:T(8,128)S(1)}, f32[72,256]{1,0:T(8,128)S(1)}, u32[]{:S(2)}, u32[]{:S(2)}) collective-permute-start(f32[72,256]{1,0:T(8,128)S(1)} %get-tuple-element.19), channel_id=1, source_target_pairs={{0,7},{1,0},{2,1},{3,2},{4,3},{5,4},{6,5},{7,6},{8,15},{9,8},{10,9... | collective-permute-start | bytes 221192 | tf_op jit(solution)/shard_map/ppermute | solution.py:308
  86.1 2.3 %collective-permute-done.14 = f32[72,256]{1,0:T(8,128)S(1)} collective-permute-done((f32[72,256]{1,0:T(8,128)S(1)}, f32[72,256]{1,0:T(8,128)S(1)}, u32[]{:S(2)}, u32[]{:S(2)}) %collective-permute-start.14) | collective-permute-done | bytes 73760 | tf_op jit(solution)/shard_map/ppermute | solution.py:308
  88.5 0.0 collective-permute-start.16
  88.5 3.5 %collective-permute-start.17 = (f32[72,256]{1,0:T(8,128)S(1)}, f32[72,256]{1,0:T(8,128)S(1)}, u32[]{:S(2)}, u32[]{:S(2)}) collective-permute-start(f32[72,256]{1,0:T(8,128)S(1)} %collective-permute-done.15), channel_id=1, source_target_pairs={{0,7},{1,0},{2,1},{3,2},{4,3},{5,4},{6,5},{7,6},{8,15},{9,8},{10,9... | collective-permute-start | bytes 221192 | tf_op jit(solution)/shard_map/ppermute | solution.py:308
  92.0 2.5 %collective-permute-done.16 = f32[72,256]{1,0:T(8,128)S(1)} collective-permute-done((f32[72,256]{1,0:T(8,128)S(1)}, f32[72,256]{1,0:T(8,128)S(1)}, u32[]{:S(2)}, u32[]{:S(2)}) %collective-permute-start.16) | collective-permute-done | bytes 73760 | tf_op jit(solution)/shard_map/ppermute | solution.py:308
  94.5 3.2 %collective-permute-start.19 = (f32[72,256]{1,0:T(8,128)S(1)}, f32[72,256]{1,0:T(8,128)S(1)}, u32[]{:S(2)}, u32[]{:S(2)}) collective-permute-start(f32[72,256]{1,0:T(8,128)S(1)} %collective-permute-done.17), channel_id=1, source_target_pairs={{0,7},{1,0},{2,1},{3,2},{4,3},{5,4},{6,5},{7,6},{8,15},{9,8},{10,9... | collective-permute-start | bytes 221192 | tf_op jit(solution)/shard_map/ppermute | solution.py:308
  97.8 2.3 %collective-permute-done.18 = f32[72,256]{1,0:T(8,128)S(1)} collective-permute-done((f32[72,256]{1,0:T(8,128)S(1)}, f32[72,256]{1,0:T(8,128)S(1)}, u32[]{:S(2)}, u32[]{:S(2)}) %collective-permute-start.18) | collective-permute-done | bytes 73760 | tf_op jit(solution)/shard_map/ppermute | solution.py:308
  100.1 0.0 collective-permute-start.20
  100.1 0.0 collective-permute-done.19
  100.1 5.5 %collective-permute-done.20 = f32[72,256]{1,0:T(8,128)S(1)} collective-permute-done((f32[72,256]{1,0:T(8,128)S(1)}, f32[72,256]{1,0:T(8,128)S(1)}, u32[]{:S(2)}, u32[]{:S(2)}) %collective-permute-start.20) | collective-permute-done | bytes 73760 | tf_op jit(solution)/shard_map/ppermute | solution.py:308
  105.6 0.3 collective-permute-start.21
  106.0 1.3 constant_dynamic-slice_fusion.1.own_ref
  107.3 0.7 collective-permute-done.21
  108.0 0.1 broadcast_select_fusion.1
  108.1 1.2 pad_maximum_fusion
  109.2 32.9 %factor.1 = (f32[512,512]{1,0:T(8,128)}, f32[8,128]{1,0:T(8,128)}) custom-call(f32[4]{0:T(128)} %pad_maximum_fusion.1.scale_ref, bf16[512,128]{1,0:T(8,128)(2,1)} %copy-done, f32[512,512]{1,0:T(8,128)} %bitcast.36), custom_call_target="tpu_custom_call" | custom-call | flops 20000000000 | bytes 4194304 | tf_op jit(solution)/shard_map/factor/pallas_call | solution.py:250
  142.1 1.2 slice.31
  143.3 0.6 maximum_bitcast_fusion.right_ref
  143.9 7.8 %reduce-scatter.2.cloned.1.call-done = f32[1,72,512]{2,1,0:T(8,128)} async-done(((f32[32,72,512]{2,1,0:T(8,128)}), f32[1,72,512]{2,1,0:T(8,128)}) %reduce-scatter.2.cloned.1.call-update) | async-done | bytes 147472 | tf_op jit(solution)/shard_map/reduce_scatter | solution.py:370
  151.7 3.6 %finish.1 = (f32[64,512]{1,0:T(8,128)}, f32[8,64]{1,0:T(8,128)}, f32[8,512]{1,0:T(8,128)}) custom-call(s32[1]{0:T(128)} %bitcast.place_ref, f32[4]{0:T(128)} %pad_maximum_fusion.1.scale_ref, bf16[64,128]{1,0:T(8,128)(2,1)} %constant_dynamic-slice_fusion.1.own_ref, bf16[512,128]{1,0:T(8,128)(2,1)} %copy-done, f32[72,512]{1,0:T(8,128)} %bitcast.38, ...), custom_call_target="tpu_custom_call" | custom-call | flops 1000000000 | bytes 2097152 | tf_op jit(solution)/shard_map/finish/pallas_call | solution.py:289
  155.3 1.2 slice_bitcast_fusion.2
  156.5 1.3 slice.30
  (21 shorter events, 0.2 us)
Async XLA Ops:
  7.2 144.5 %reduce-scatter.2.cloned.1.call-start = ((), (), s32[]{:S(2)}) async-start(), calls=%async_computation.1 | async-start | bytes 4866048 | tf_op jit(solution)/shard_map/reduce_scatter | solution.py:370
  8.1 12.5 %collective-permute-start = (bf16[512,128]{1,0:T(8,128)(2,1)S(1)}, bf16[512,128]{1,0:T(8,128)(2,1)S(1)}, u32[]{:S(2)}, u32[]{:S(2)}) collective-permute-start(bf16[512,128]{1,0:T(8,128)(2,1)S(1)} %slice.24), channel_id=1, source_target_pairs={{0,7},{8,15},{16,23},{24,31},{32,39},{40,47},{48,55},{56,63},{64,7... | collective-permute-start | bytes 393224 | tf_op jit(solution)/shard_map/ppermute | solution.py:360
  14.2 7.8 %collective-permute-start.1 = (bf16[512,128]{1,0:T(8,128)(2,1)S(1)}, bf16[512,128]{1,0:T(8,128)(2,1)S(1)}, u32[]{:S(2)}, u32[]{:S(2)}) collective-permute-start(bf16[512,128]{1,0:T(8,128)(2,1)S(1)} %slice.24), channel_id=1, source_target_pairs={{0,6},{8,14},{16,22},{24,30},{32,38},{40,46},{48,54},{56,62},{64,7... | collective-permute-start | bytes 393224 | tf_op jit(solution)/shard_map/ppermute | solution.py:360
  15.5 23.8 %collective-permute-start.2 = (bf16[512,128]{1,0:T(8,128)(2,1)S(1)}, bf16[512,128]{1,0:T(8,128)(2,1)S(1)}, u32[]{:S(2)}, u32[]{:S(2)}) collective-permute-start(bf16[512,128]{1,0:T(8,128)(2,1)S(1)} %slice.24), channel_id=1, source_target_pairs={{0,5},{8,13},{16,21},{24,29},{32,37},{40,45},{48,53},{56,61},{64,6... | collective-permute-start | bytes 393224 | tf_op jit(solution)/shard_map/ppermute | solution.py:360
  16.8 22.5 %collective-permute-start.3 = (bf16[512,128]{1,0:T(8,128)(2,1)S(1)}, bf16[512,128]{1,0:T(8,128)(2,1)S(1)}, u32[]{:S(2)}, u32[]{:S(2)}) collective-permute-start(bf16[512,128]{1,0:T(8,128)(2,1)S(1)} %slice.24), channel_id=1, source_target_pairs={{0,4},{8,12},{16,20},{24,28},{32,36},{40,44},{48,52},{56,60},{64,6... | collective-permute-start | bytes 393224 | tf_op jit(solution)/shard_map/ppermute | solution.py:360
  18.1 21.2 %collective-permute-start.4 = (bf16[512,128]{1,0:T(8,128)(2,1)S(1)}, bf16[512,128]{1,0:T(8,128)(2,1)S(1)}, u32[]{:S(2)}, u32[]{:S(2)}) collective-permute-start(bf16[512,128]{1,0:T(8,128)(2,1)S(1)} %slice.24), channel_id=1, source_target_pairs={{0,3},{8,11},{16,19},{24,27},{32,35},{40,43},{48,51},{56,59},{64,6... | collective-permute-start | bytes 393224 | tf_op jit(solution)/shard_map/ppermute | solution.py:360
  20.7 18.6 %collective-permute-start.5 = (bf16[512,128]{1,0:T(8,128)(2,1)S(1)}, bf16[512,128]{1,0:T(8,128)(2,1)S(1)}, u32[]{:S(2)}, u32[]{:S(2)}) collective-permute-start(bf16[512,128]{1,0:T(8,128)(2,1)S(1)} %slice.24), channel_id=1, source_target_pairs={{0,2},{8,10},{16,18},{24,26},{32,34},{40,42},{48,50},{56,58},{64,6... | collective-permute-start | bytes 393224 | tf_op jit(solution)/shard_map/ppermute | solution.py:360
  22.0 17.3 %collective-permute-start.6 = (bf16[512,128]{1,0:T(8,128)(2,1)S(1)}, bf16[512,128]{1,0:T(8,128)(2,1)S(1)}, u32[]{:S(2)}, u32[]{:S(2)}) collective-permute-start(bf16[512,128]{1,0:T(8,128)(2,1)S(1)} %slice.24), channel_id=1, source_target_pairs={{0,1},{8,9},{16,17},{24,25},{32,33},{40,41},{48,49},{56,57},{64,65... | collective-permute-start | bytes 393224 | tf_op jit(solution)/shard_map/ppermute | solution.py:360
  23.3 14.3 %copy-start.2 = (bf16[2048]{0:T(1024)(128)(2,1)S(1)}, bf16[2048]{0:T(1024)(128)(2,1)}, u32[]{:S(2)}) copy-start(bf16[2048]{0:T(1024)(128)(2,1)} %param.12) | copy-start | bytes 12292
  40.3 1.3 copy-start
  61.3 0.9 copy-start.1
  62.2 1.4 collective-permute-start.7
  63.6 5.1 %collective-permute-start.10 = (f32[72,256]{1,0:T(8,128)S(1)}, f32[72,256]{1,0:T(8,128)S(1)}, u32[]{:S(2)}, u32[]{:S(2)}) collective-permute-start(f32[72,256]{1,0:T(8,128)S(1)} %fusion.4), channel_id=1, source_target_pairs={{0,48},{8,56},{16,0},{24,8},{32,16},{40,24},{48,32},{56,40},{64,11... | collective-permute-start | bytes 221192 | tf_op jit(solution)/shard_map/ppermute | solution.py:308
  66.4 6.8 %collective-permute-start.8 = (f32[72,256]{1,0:T(8,128)S(1)}, f32[72,256]{1,0:T(8,128)S(1)}, u32[]{:S(2)}, u32[]{:S(2)}) collective-permute-start(f32[72,256]{1,0:T(8,128)S(1)} %fusion.4), channel_id=1, source_target_pairs={{0,16},{8,24},{16,32},{24,40},{32,48},{40,56},{48,0},{56,8},{64,80... | collective-permute-start | bytes 221192 | tf_op jit(solution)/shard_map/ppermute | solution.py:308
  66.4 6.8 %collective-permute-start.9 = (f32[72,256]{1,0:T(8,128)S(1)}, f32[72,256]{1,0:T(8,128)S(1)}, u32[]{:S(2)}, u32[]{:S(2)}) collective-permute-start(f32[72,256]{1,0:T(8,128)S(1)} %fusion.4), channel_id=1, source_target_pairs={{0,32},{8,40},{16,48},{24,56},{32,0},{40,8},{48,16},{56,24},{64,96... | collective-permute-start | bytes 221192 | tf_op jit(solution)/shard_map/ppermute | solution.py:308
  73.3 5.3 %collective-permute-start.13 = (f32[72,256]{1,0:T(8,128)S(1)}, f32[72,256]{1,0:T(8,128)S(1)}, u32[]{:S(2)}, u32[]{:S(2)}) collective-permute-start(f32[72,256]{1,0:T(8,128)S(1)} %add_add_fusion.1), channel_id=1, source_target_pairs={{0,192},{8,200},{16,208},{24,216},{32,224},{40,232},{48,240},{56,2... | collective-permute-start | bytes 221192 | tf_op jit(solution)/shard_map/ppermute | solution.py:308
  76.4 6.4 %collective-permute-start.11 = (f32[72,256]{1,0:T(8,128)S(1)}, f32[72,256]{1,0:T(8,128)S(1)}, u32[]{:S(2)}, u32[]{:S(2)}) collective-permute-start(f32[72,256]{1,0:T(8,128)S(1)} %add_add_fusion.1), channel_id=1, source_target_pairs={{0,64},{8,72},{16,80},{24,88},{32,96},{40,104},{48,112},{56,120},{... | collective-permute-start | bytes 221192 | tf_op jit(solution)/shard_map/ppermute | solution.py:308
  76.4 6.4 %collective-permute-start.12 = (f32[72,256]{1,0:T(8,128)S(1)}, f32[72,256]{1,0:T(8,128)S(1)}, u32[]{:S(2)}, u32[]{:S(2)}) collective-permute-start(f32[72,256]{1,0:T(8,128)S(1)} %add_add_fusion.1), channel_id=1, source_target_pairs={{0,128},{8,136},{16,144},{24,152},{32,160},{40,168},{48,176},{56,1... | collective-permute-start | bytes 221192 | tf_op jit(solution)/shard_map/ppermute | solution.py:308
  82.8 5.6 %collective-permute-start.14 = (f32[72,256]{1,0:T(8,128)S(1)}, f32[72,256]{1,0:T(8,128)S(1)}, u32[]{:S(2)}, u32[]{:S(2)}) collective-permute-start(f32[72,256]{1,0:T(8,128)S(1)} %get-tuple-element.19), channel_id=1, source_target_pairs={{0,1},{1,2},{2,3},{3,4},{4,5},{5,6},{6,7},{7,0},{8,9},{9,10},{10,1... | collective-permute-start | bytes 221192 | tf_op jit(solution)/shard_map/ppermute | solution.py:308
  82.9 5.6 %collective-permute-start.15 = (f32[72,256]{1,0:T(8,128)S(1)}, f32[72,256]{1,0:T(8,128)S(1)}, u32[]{:S(2)}, u32[]{:S(2)}) collective-permute-start(f32[72,256]{1,0:T(8,128)S(1)} %get-tuple-element.19), channel_id=1, source_target_pairs={{0,7},{1,0},{2,1},{3,2},{4,3},{5,4},{6,5},{7,6},{8,15},{9,8},{10,9... | collective-permute-start | bytes 221192 | tf_op jit(solution)/shard_map/ppermute | solution.py:308
  88.5 6.0 %collective-permute-start.16 = (f32[72,256]{1,0:T(8,128)S(1)}, f32[72,256]{1,0:T(8,128)S(1)}, u32[]{:S(2)}, u32[]{:S(2)}) collective-permute-start(f32[72,256]{1,0:T(8,128)S(1)} %collective-permute-done.14), channel_id=1, source_target_pairs={{0,1},{1,2},{2,3},{3,4},{4,5},{5,6},{6,7},{7,0},{8,9},{9,10},{10,1... | collective-permute-start | bytes 221192 | tf_op jit(solution)/shard_map/ppermute | solution.py:308
  88.5 6.0 %collective-permute-start.17 = (f32[72,256]{1,0:T(8,128)S(1)}, f32[72,256]{1,0:T(8,128)S(1)}, u32[]{:S(2)}, u32[]{:S(2)}) collective-permute-start(f32[72,256]{1,0:T(8,128)S(1)} %collective-permute-done.15), channel_id=1, source_target_pairs={{0,7},{1,0},{2,1},{3,2},{4,3},{5,4},{6,5},{7,6},{8,15},{9,8},{10,9... | collective-permute-start | bytes 221192 | tf_op jit(solution)/shard_map/ppermute | solution.py:308
  94.5 5.6 %collective-permute-start.18 = (f32[72,256]{1,0:T(8,128)S(1)}, f32[72,256]{1,0:T(8,128)S(1)}, u32[]{:S(2)}, u32[]{:S(2)}) collective-permute-start(f32[72,256]{1,0:T(8,128)S(1)} %collective-permute-done.16), channel_id=1, source_target_pairs={{0,1},{1,2},{2,3},{3,4},{4,5},{5,6},{6,7},{7,0},{8,9},{9,10},{10,1... | collective-permute-start | bytes 221192 | tf_op jit(solution)/shard_map/ppermute | solution.py:308
  94.5 5.6 %collective-permute-start.19 = (f32[72,256]{1,0:T(8,128)S(1)}, f32[72,256]{1,0:T(8,128)S(1)}, u32[]{:S(2)}, u32[]{:S(2)}) collective-permute-start(f32[72,256]{1,0:T(8,128)S(1)} %collective-permute-done.17), channel_id=1, source_target_pairs={{0,7},{1,0},{2,1},{3,2},{4,3},{5,4},{6,5},{7,6},{8,15},{9,8},{10,9... | collective-permute-start | bytes 221192 | tf_op jit(solution)/shard_map/ppermute | solution.py:308
  100.1 5.6 %collective-permute-start.20 = (f32[72,256]{1,0:T(8,128)S(1)}, f32[72,256]{1,0:T(8,128)S(1)}, u32[]{:S(2)}, u32[]{:S(2)}) collective-permute-start(f32[72,256]{1,0:T(8,128)S(1)} %collective-permute-done.18), channel_id=1, source_target_pairs={{0,1},{1,2},{2,3},{3,4},{4,5},{5,6},{6,7},{7,0},{8,9},{9,10},{10,1... | collective-permute-start | bytes 221192 | tf_op jit(solution)/shard_map/ppermute | solution.py:308
  105.6 2.3 %collective-permute-start.21 = (f32[8,72,256]{2,1,0:T(8,128)S(1)}, f32[8,72,256]{2,1,0:T(8,128)S(1)}, u32[]{:S(2)}, u32[]{:S(2)}) collective-permute-start(f32[8,72,256]{2,1,0:T(8,128)S(1)} %bitcast_dynamic-update-slice_fusion), channel_id=1, source_target_pairs={{0,8},{8,0},{16,24},{24,16},{32,40},{40,32},{48,56},{56,48},{64,72... | collective-permute-start | bytes 1769480 | tf_op jit(solution)/shard_map/ppermute | solution.py:308
Sparse Core Ops, SparseCore 0:
  61.4 90.2 reduce-scatter.1
